TPU v7x, 32 devices: a whole 2x2x4 slice. The times are simulated.
32 devices in a mesh: study: 2 (over x), vol: 8 (over z, y), tile: 2 (over core).
Axes of the slice: x: 2, y: 2, z: 4, core: 2. Of those that a mesh axis runs over, the one named last changes fastest.
Arguments:
- spectra: bfloat16 [16, 4, 768, 2048], P(('study', 'vol'), None, 'tile'), parts along dimension 0, may hold values from -6 to 6
- block_scales: float32 [16, 4, 768, 16], P(('study', 'vol'), None, 'tile'), parts along dimension 0, may hold values from 0.3 to 3
- retina_blocks: int32 [12, 2], P(('study', 'tile')), parts along dimension 0, may hold values from 0 to 3, as said below
- quality_block: int32 [16, 6], P(('study', 'vol'), 'tile'), parts along dimension 0, may hold values from 0 to 3, as said below
- quality_bias: float32 [16, 6], P(('study', 'vol'), 'tile'), parts along dimension 0, may hold values from -110 to 160
Outputs:
- angiogram: float32 [1024, 768], P(('study', 'vol'), 'tile'), parts along dimension 0
- joined_structure: float32 [1024, 768], P(('study', 'vol'), 'tile'), parts along dimension 0
- spread_map: float32 [1024, 768], P(('study', 'vol'), 'tile'), parts along dimension 0
There are 2 independent parts, one for each index of `study`. A program takes and returns all parts, laid end to end along the dimension named above; each array names one. Nothing has to cross between parts.
Inputs may be any that keep to these rules, and one draw needn't show every extreme that they name: retina_blocks[j,0] <= retina_blocks[j,1]. quality_block[v,j] lies between retina_blocks[j,0] and retina_blocks[j,1].
All inputs are finite; a program needn't handle non-finite values.
Results may differ from a plain program's by a relative error of at most 0.0015.
Values sent between devices are 32-bit elements; how exact they have to be, the bound alone decides.
A program may use at most 128 MiB of HBM per device.

v0:
```python
import functools
import math

import jax
import jax.numpy as jnp
from jax import lax
from jax.experimental import pallas as pl
from jax.experimental.pallas import tpu as pltpu
from jax.sharding import PartitionSpec as P

DEPTH = 512
BANDS = 4
DBLK = 128
ABLK = 128
SB = 128
NDB = 4
CLASSES = 8
MESH = pl.DeviceIdType.MESH
ZR = 136


def build_tables(table, perm, samples):
    inner = samples // CLASSES
    z = lax.broadcasted_iota(jnp.int32, (ZR, inner), 0)
    k1 = lax.broadcasted_iota(jnp.int32, (ZR, inner), 1)
    unit = 2.0 * math.pi / samples
    base = ((CLASSES * k1 * z) % samples).astype(jnp.float32) * unit
    step = z.astype(jnp.float32) * unit
    re, im = jnp.cos(base), -jnp.sin(base)
    sre, sim = jnp.cos(step), -jnp.sin(step)
    kk = (
        lax.broadcasted_iota(jnp.int32, (CLASSES, inner), 1) * CLASSES
        + lax.broadcasted_iota(jnp.int32, (CLASSES, inner), 0)
    ).astype(jnp.float32)
    windows = []
    for b in range(BANDS):
        distance = kk - (b + 0.5) * (samples / BANDS)
        offset = distance / (samples / 8.0)
        g = jnp.where(jnp.abs(distance) <= samples / 2.0, jnp.exp(-0.5 * offset * offset), 0.0)
        windows.append(g / jnp.sqrt(jnp.sum(g * g, keepdims=True)))
    for k0 in range(CLASSES):
        if k0:
            re, im = re * sre - im * sim, re * sim + im * sre
        both = jnp.concatenate([re, im], axis=0)
        for b in range(BANDS):
            row = windows[b][k0 : k0 + 1, :]
            table[k0, b * 2 * ZR : (b + 1) * 2 * ZR, :] = (both * row).astype(jnp.bfloat16)
    size = perm.shape[0]
    part = size // CLASSES
    row = lax.broadcasted_iota(jnp.int32, (size, size), 0)
    col = lax.broadcasted_iota(jnp.int32, (size, size), 1)
    perm[...] = jnp.where(col == (row % part) * CLASSES + row // part, 1.0, 0.0).astype(jnp.bfloat16)


def combine(get):
    rr, ii = [get(k, 0) for k in range(8)], [get(k, 1) for k in range(8)]
    sr = [rr[j] + rr[j + 4] for j in range(4)]
    si = [ii[j] + ii[j + 4] for j in range(4)]
    dr = [rr[j] - rr[j + 4] for j in range(4)]
    di = [ii[j] - ii[j + 4] for j in range(4)]
    half = math.sqrt(0.5)
    re0, im0 = (sr[0] + sr[2]) + (sr[1] + sr[3]), (si[0] + si[2]) + (si[1] + si[3])
    re3, im3 = (sr[0] - sr[2]) - (si[1] - si[3]), (si[0] - si[2]) + (sr[1] - sr[3])
    p, q = (dr[1] - dr[3]) * half, (di[1] + di[3]) * half
    r, t = (di[1] - di[3]) * half, (dr[1] + dr[3]) * half
    re2, im2 = (dr[0] + di[2]) + (p + q), (di[0] - dr[2]) + (r - t)
    re1, im1 = (dr[0] - di[2]) + (p - q), (di[0] + dr[2]) + (r + t)
    fields = ((re0, im0), (re1, im1), (re2, im2), (re3, im3))
    return [re * re + (im * im + 0.05) for re, im in fields]


def fused_kernel(
    retina, qblock, bias, spec, scales, joined_out,
    table, perm, data, ga, gb, acc_ratio, acc_power,
    sent, got, score_sent, score_got, part_sent, part_got, part_near, redge,
    ssem, rsem, csem, dsem, psem, qsem, lsem, esem,
):
    j = pl.program_id(0)
    repeats, lines, samples = spec.shape[1:]
    chunk = perm.shape[0]
    tiles, n = score_got.shape[:2]
    half = n // 2
    rows = redge.shape[2]
    me, t = lax.axis_index("vol"), lax.axis_index("tile")
    other = 1 - t
    side, place = me // half, me % half
    here = tile_at(j, tiles)
    part = chunk // CLASSES
    cols = repeats * lines

    @pl.when(j == 0)
    def _():
        barrier = pltpu.get_barrier_semaphore()
        for d in range(1, n):
            pl.semaphore_signal(
                barrier, inc=1, device_id={"vol": (me + d) % n}, device_id_type=MESH
            )
        pl.semaphore_signal(barrier, inc=1, device_id={"tile": other}, device_id_type=MESH)
        build_tables(table, perm, samples)

    scale_t = jnp.concatenate([scales[0, r] for r in range(repeats)], axis=1)
    for q in range(samples // chunk):
        block = spec[0, :, :, q * chunk : (q + 1) * chunk].reshape(cols, chunk)
        moved = lax.dot_general(
            perm[...], block, (((1,), (1,)), ((), ())), preferred_element_type=jnp.float32
        )
        per = chunk // SB
        factor = jnp.concatenate(
            [
                jnp.broadcast_to(scale_t[q * per + h : q * per + h + 1, :], (part // per, cols))
                for h in range(per)
            ],
            axis=0,
        )
        for k0 in range(CLASSES):
            data[k0, q * part : (q + 1) * part, :] = (
                moved[k0 * part : (k0 + 1) * part] * factor
            ).astype(jnp.bfloat16)

    buffers = (ga, gb)

    def multiply(b, classes):
        for k0 in classes:
            buffers[b % 2][k0] = jnp.dot(
                table[k0, b * 2 * ZR : (b + 1) * 2 * ZR, :],
                data[k0],
                preferred_element_type=jnp.float32,
            )

    def reduce(b, groups):
        g = buffers[b % 2]

        for i in groups:
            at = i * 8
            powers = []
            for r in range(repeats):
                def get(k, c):
                    return g[k, c * ZR + at : c * ZR + at + 8, r * lines : (r + 1) * lines]

                powers.append(combine(get))
            for d in range(NDB):
                total = powers[0][d]
                ratio = None
                for r in range(repeats - 1):
                    first, second = powers[r][d], powers[r + 1][d]
                    total = total + second
                    prod, both = first * second, first + second
                    term = prod * lax.rsqrt(prod * (both * both))
                    ratio = term if ratio is None else ratio + term
                if b:
                    total = total + acc_power[d, at : at + 8, :]
                    ratio = ratio + acc_ratio[d, at : at + 8, :]
                acc_power[d, at : at + 8, :] = total
                acc_ratio[d, at : at + 8, :] = ratio

    multiply(0, range(CLASSES))
    groups = ZR // 8
    for b in range(BANDS):
        for k0 in range(CLASSES):
            if b + 1 < BANDS:
                multiply(b + 1, (k0,))
            reduce(b, range(k0 * groups // CLASSES, (k0 + 1) * groups // CLASSES))

    flip = jnp.where(
        lax.broadcasted_iota(jnp.int32, (DBLK, ZR), 0)
        + lax.broadcasted_iota(jnp.int32, (DBLK, ZR), 1)
        == DBLK,
        1.0,
        0.0,
    )
    first, last, rated = retina[0, here], retina[1, here], qblock[0, here]
    score = jnp.zeros((1, lines), jnp.float32)
    for d in range(NDB):
        ratio, power = acc_ratio[d], acc_power[d]
        dec = 1.0 - ratio * (2.0 / (BANDS * (repeats - 1)))
        struct = jnp.log(power * (1.0 / (BANDS * repeats)) + 0.05)
        if d % 2:
            dec = jnp.dot(flip, dec, precision=lax.Precision.HIGHEST)
            struct = jnp.dot(flip, struct, precision=lax.Precision.HIGHEST)
        else:
            dec, struct = dec[:DBLK], struct[:DBLK]
        inside = (first <= d) & (d <= last)
        score = score + jnp.where(rated == d, jnp.sum(struct, axis=0, keepdims=True), 0.0)
        dec, struct = jnp.where(inside, dec, 0.0), jnp.where(inside, struct, 0.0)
        per = DBLK // rows
        for s in range(per):
            u = d * per + s
            sent[j, u % half, u // half, :rows, :] = dec[s * rows : (s + 1) * rows]
            sent[j, u % half, u // half, rows:, :] = struct[s * rows : (s + 1) * rows]
    mean = jnp.sum(score, axis=1, keepdims=True) * (1.0 / (DBLK * lines)) + bias[0, here]
    score_sent[j] = jnp.broadcast_to(mean, (8, lines))

    def maps(step, d):
        target = (place + d) % half
        return pltpu.make_async_remote_copy(
            src_ref=sent.at[step, target], dst_ref=got.at[step, place],
            send_sem=ssem.at[step, d], recv_sem=rsem.at[step, d],
            device_id={"vol": side * half + target}, device_id_type=MESH,
        )

    def scores(step, d):
        return pltpu.make_async_remote_copy(
            src_ref=score_sent.at[step], dst_ref=score_got.at[step, me],
            send_sem=csem.at[step, d], recv_sem=dsem.at[step, d],
            device_id={"vol": (me + d) % n}, device_id_type=MESH,
        )

    def partial(step):
        return pltpu.make_async_remote_copy(
            src_ref=part_sent.at[step], dst_ref=part_got.at[step],
            send_sem=psem.at[step], recv_sem=qsem.at[step],
            device_id={"vol": (1 - side) * half + place}, device_id_type=MESH,
        )

    def own_maps(step):
        return pltpu.make_async_copy(sent.at[step, place], got.at[step, place], lsem.at[0, step])

    def own_score(step):
        return pltpu.make_async_copy(score_sent.at[step], score_got.at[step, me], lsem.at[1, step])

    @pl.when(j == 0)
    def _():
        pl.semaphore_wait(pltpu.get_barrier_semaphore(), n)

    for d in range(1, n):
        scores(j, d).start()
    for d in range(1, half):
        maps(j, d).start()
    own_maps(j).start()
    own_score(j).start()

    @pl.when(j == tiles - 1)
    def _():
        lane = lax.broadcasted_iota(jnp.int32, (rows, lines), 1)
        middle = lines // 2
        inner = (lane >= middle * t) & (lane < middle + middle * t)

        def arrive(step):
            own_maps(step).wait()
            own_score(step).wait()
            for d in range(1, n):
                scores(step, d).wait_recv()
            for d in range(1, half):
                maps(step, d).wait_recv()

        def add_up(step):
            ratings = [score_got[step, v, :1, :] for v in range(n)]
            top = functools.reduce(jnp.maximum, ratings)
            total = functools.reduce(jnp.add, [jnp.exp(x - top) for x in ratings])
            weights = [
                jnp.exp(score_got[step, side * half + v, :1, :] - top) / total
                for v in range(half)
            ]
            for far in range(2):
                to = 1 - side if far else side
                ang = square = joined = jnp.zeros((rows, lines), jnp.float32)
                for v in range(half):
                    own = got[step, v, to, :rows, :]
                    if step + 1 < tiles:
                        after = got[step + 1, v, to, :rows, :]
                    else:
                        after = redge[v, to]
                    before = got[step - 1, v, to, :rows, :] if step else 0.0
                    near = jnp.where(inner, after, before)
                    right2 = pltpu.roll(jnp.where(lane >= lines - 2, near, own), 2, 1)
                    right1 = pltpu.roll(jnp.where(lane >= lines - 1, near, own), 1, 1)
                    left1 = pltpu.roll(jnp.where(lane < 1, near, own), lines - 1, 1)
                    left2 = pltpu.roll(jnp.where(lane < 2, near, own), lines - 2, 1)
                    smooth = (
                        (right2 + left2) * (1.0 / 9.0)
                        + (right1 + left1) * (2.0 / 9.0)
                        + own * (3.0 / 9.0)
                    )
                    ws = weights[v] * smooth
                    ang = ang + ws
                    square = square + ws * smooth
                    joined = joined + weights[v] * got[step, v, to, rows:, :]
                store = part_sent if far else part_near
                store[step, 0] = ang
                store[step, 1] = square
                store[step, 2] = joined
            partial(step).start()

        edge = pltpu.make_async_remote_copy(
            src_ref=got.at[tiles - 1, :, :, pl.ds(0, rows), :], dst_ref=redge,
            send_sem=esem.at[0], recv_sem=esem.at[1],
            device_id={"tile": other}, device_id_type=MESH,
        )
        arrive(0)
        for step in range(tiles):
            if step + 1 < tiles:
                arrive(step + 1)
            if step + 1 == max(tiles - 1, 1):
                edge.start()
            if step + 1 == tiles:
                edge.wait_recv()
            add_up(step)
        for step in range(tiles):
            partial(step).wait_recv()
            at = pl.ds(pl.multiple_of(tile_at(step, tiles) * lines, lines), lines)
            for k in range(3):
                joined_out[k, :, at] = part_near[step, k] + part_got[step, k]
        for step in range(tiles):
            partial(step).wait_send()
            for d in range(1, n):
                scores(step, d).wait_send()
            for d in range(1, half):
                maps(step, d).wait_send()
        edge.wait_send()


def tile_at(step, tiles):
    t = lax.axis_index("tile")
    return step + t * (tiles - 1 - 2 * step)


def fused(n, spectra, block_scales, retina, qblock, bias):
    _, repeats, lines, samples = spectra.shape
    kb = block_scales.shape[3]
    tiles = lines // ABLK
    inner = samples // CLASSES
    cols = repeats * ABLK
    rows = DEPTH // n
    smem = pl.BlockSpec(memory_space=pltpu.SMEM)
    return pl.pallas_call(
        fused_kernel,
        grid=(tiles,),
        out_shape=jax.ShapeDtypeStruct((3, rows, lines), jnp.float32),
        in_specs=[
            smem, smem, smem,
            pl.BlockSpec((1, repeats, ABLK, samples), lambda j: (0, 0, tile_at(j, tiles), 0)),
            pl.BlockSpec((1, repeats, kb, ABLK), lambda j: (0, 0, 0, tile_at(j, tiles))),
        ],
        out_specs=pl.BlockSpec((3, rows, lines), lambda j: (0, 0, 0)),
        scratch_shapes=[
            pltpu.VMEM((CLASSES, BANDS * 2 * ZR, inner), jnp.bfloat16),
            pltpu.VMEM((256, 256), jnp.bfloat16),
            pltpu.VMEM((CLASSES, inner, cols), jnp.bfloat16),
            pltpu.VMEM((CLASSES, 2 * ZR, cols), jnp.float32),
            pltpu.VMEM((CLASSES, 2 * ZR, cols), jnp.float32),
            pltpu.VMEM((NDB, ZR, ABLK), jnp.float32),
            pltpu.VMEM((NDB, ZR, ABLK), jnp.float32),
            pltpu.VMEM((tiles, n // 2, 2, 2 * rows, ABLK), jnp.float32),
            pltpu.VMEM((tiles, n // 2, 2, 2 * rows, ABLK), jnp.float32),
            pltpu.VMEM((tiles, 8, ABLK), jnp.float32),
            pltpu.VMEM((tiles, n, 8, ABLK), jnp.float32),
            pltpu.VMEM((tiles, 3, rows, ABLK), jnp.float32),
            pltpu.VMEM((tiles, 3, rows, ABLK), jnp.float32),
            pltpu.VMEM((tiles, 3, rows, ABLK), jnp.float32),
            pltpu.VMEM((n // 2, 2, rows, ABLK), jnp.float32),
            pltpu.SemaphoreType.DMA((tiles, n // 2)),
            pltpu.SemaphoreType.DMA((tiles, n // 2)),
            pltpu.SemaphoreType.DMA((tiles, n)),
            pltpu.SemaphoreType.DMA((tiles, n)),
            pltpu.SemaphoreType.DMA((tiles,)),
            pltpu.SemaphoreType.DMA((tiles,)),
            pltpu.SemaphoreType.DMA((2, tiles)),
            pltpu.SemaphoreType.DMA((2,)),
        ],
        compiler_params=pltpu.CompilerParams(
            vmem_limit_bytes=67043328, collective_id=0, has_side_effects=True
        ),
    )(retina.T, qblock, bias, spectra, block_scales.transpose(0, 1, 3, 2))


def finish_kernel(joined, ang_out, str_out, spread_out):
    ang = joined[0]
    ang_out[...] = ang
    str_out[...] = joined[2]
    spread_out[...] = jnp.sqrt(joined[1] - ang * ang + 0.01)


def finish(joined):
    out = jax.ShapeDtypeStruct(joined.shape[1:], jnp.float32)
    return pl.pallas_call(finish_kernel, out_shape=(out, out, out))(joined)


def solution(mesh):
    n = mesh.shape["vol"]
    assert mesh.shape["tile"] == 2

    def on_device(spectra, block_scales, retina_blocks, quality_block, quality_bias):
        return finish(
            fused(n, spectra, block_scales, retina_blocks, quality_block, quality_bias)
        )

    return jax.shard_map(
        on_device,
        mesh=mesh,
        in_specs=(
            P(("study", "vol"), None, "tile", None),
            P(("study", "vol"), None, "tile", None),
            P(("study", "tile"), None),
            P(("study", "vol"), "tile"),
            P(("study", "vol"), "tile"),
        ),
        out_specs=(
            P(("study", "vol"), "tile"),
            P(("study", "vol"), "tile"),
            P(("study", "vol"), "tile"),
        ),
        check_vma=False,
    )
```

profile of v0, /device:TPU:0, one launch (start us, length us, event | category | flops | bytes accessed | tf_op | source)
XLA Modules:
  0.0 50.1 jit_solution(14853203450378930727)
XLA Ops:
  0.6 47.7 %shard_map.76.joined = f32[3,64,384]{2,1,0:T(8,128)} custom-call(s32[2,3]{1,0:T(2,128)} %bitcast.3, s32[1,3]{1,0:T(1,128)} %qblock.1, f32[1,3]{1,0:T(1,128)} %bias.1, bf16[1,4,384,2048]{3,2,1,0:T(8,128)(2,1)} %spec.1, f32[1,4,16,384]{3,2,1,0:T(8,128)} %bitcast.2), custom_call_target="tpu_custom_call" | custom-call | tf_op jit(solution)/shard_map/pallas_call | solution.py:325
  48.4 1.7 %shard_map.77 = (f32[64,384]{1,0:T(8,128)}, f32[64,384]{1,0:T(8,128)}, f32[64,384]{1,0:T(8,128)}) custom-call(f32[3,64,384]{2,1,0:T(8,128)} %shard_map.76.joined), custom_call_target="tpu_custom_call" | custom-call | tf_op jit(solution)/shard_map/pallas_call | solution.py:375
where the time goes:
time: 50.2 us; the launch traced here: 50.1 us
  Pallas kernels  49.4 us (98%)
  between operations  0.64 us (1%)
    pallas_call x1, Pallas kernels, fused(): pl.pallas_call(fused_kernel, grid=(tiles,), out_shape=jax.ShapeDtypeStruc...  47.7 us
    pallas_call x1, Pallas kernels, finish(): return pl.pallas_call(finish_kernel, out_shape=(out, out, out))(joined)  1.67 us

commit v1 on v0

v1 whole, which is shorter than its diff:
```python
import functools
import math

import jax
import jax.numpy as jnp
from jax import lax
from jax.experimental import pallas as pl
from jax.experimental.pallas import tpu as pltpu
from jax.sharding import PartitionSpec as P

DEPTH = 512
BANDS = 4
DBLK = 128
ABLK = 128
SB = 128
NDB = 4
CLASSES = 8
MESH = pl.DeviceIdType.MESH
PART = 32
PARTS = DBLK // PART
GROUPS = PART // 8
UNROLL = 4
SPREAD = 2
HEAD = BANDS * 2 * PART
LHS = HEAD + 16


def turn(re, im, cre, cim):
    return re * cre - im * cim, re * cim + im * cre


def build_trig(wins, trig, steps, perm, samples):
    inner = samples // CLASSES
    unit = 2.0 * math.pi / samples
    kk = (
        lax.broadcasted_iota(jnp.int32, (CLASSES, inner), 1) * CLASSES
        + lax.broadcasted_iota(jnp.int32, (CLASSES, inner), 0)
    ).astype(jnp.float32)
    for k0 in range(CLASSES):
        wins[k0] = jnp.zeros((8, inner), jnp.float32)
    for b in range(BANDS):
        distance = kk - (b + 0.5) * (samples / BANDS)
        offset = distance / (samples / 8.0)
        g = jnp.where(jnp.abs(distance) <= samples / 2.0, jnp.exp(-0.5 * offset * offset), 0.0)
        g = g / jnp.sqrt(jnp.sum(g * g, keepdims=True))
        for k0 in range(CLASSES):
            wins[k0, b : b + 1, :] = g[k0 : k0 + 1]
    z = lax.broadcasted_iota(jnp.int32, (8, inner), 0)
    k1 = lax.broadcasted_iota(jnp.int32, (8, inner), 1)
    angle = ((CLASSES * k1 * z) % samples).astype(jnp.float32) * unit
    trig[0, :8], trig[1, :8] = jnp.cos(angle), -jnp.sin(angle)
    angle = ((CLASSES * k1 * 8) % samples).astype(jnp.float32) * unit
    cre, cim = jnp.cos(angle), -jnp.sin(angle)
    angle = z.astype(jnp.float32)[:, :128] * unit
    steps[0, :8], steps[1, :8] = jnp.cos(angle), -jnp.sin(angle)
    have = 8
    while have < DBLK:
        for at in range(0, have, 8):
            to = pl.ds(have + at, 8)
            trig[0, to], trig[1, to] = turn(trig[0, at : at + 8], trig[1, at : at + 8], cre, cim)
            steps[0, to], steps[1, to] = turn(
                steps[0, at : at + 8],
                steps[1, at : at + 8],
                math.cos(have * unit),
                -math.sin(have * unit),
            )
        cre, cim = turn(cre, cim, cre, cim)
        have *= 2
    last = pl.ds(DBLK, 8)
    trig[0, last], trig[1, last] = cre, cim
    steps[0, last] = jnp.full((8, 128), math.cos(DBLK * unit), jnp.float32)
    steps[1, last] = jnp.full((8, 128), -math.sin(DBLK * unit), jnp.float32)
    size = perm.shape[0]
    part = size // CLASSES
    row = lax.broadcasted_iota(jnp.int32, (size, size), 0)
    col = lax.broadcasted_iota(jnp.int32, (size, size), 1)
    perm[...] = jnp.where(col == (row % part) * CLASSES + row // part, 1.0, 0.0).astype(jnp.bfloat16)


def build_class(table, wins, trig, steps, k0):
    inner = trig.shape[2]
    rows = [wins[k0, b : b + 1, :] for b in range(BANDS)]
    for p in range(PARTS):
        at = pl.ds(p * PART, PART)
        for c in range(2):
            value = trig[c, at]
            for b in range(BANDS):
                to = pl.ds((b * 2 + c) * PART, PART)
                table[p, k0, to, :] = (value * rows[b]).astype(jnp.bfloat16)
    last = pl.ds(DBLK, 8)
    both = jnp.concatenate([trig[c, last] * wins[k0] for c in range(2)], axis=0)
    for p in range(PARTS):
        table[p, k0, HEAD:LHS, :] = both.astype(jnp.bfloat16)
    for at in range(0, DBLK + 8, 8):
        here = pl.ds(at, 8)
        sre = jnp.concatenate([steps[0, here]] * (inner // 128), axis=1)
        sim = jnp.concatenate([steps[1, here]] * (inner // 128), axis=1)
        trig[0, here], trig[1, here] = turn(trig[0, here], trig[1, here], sre, sim)


def combine(get):
    rr, ii = [get(k, 0) for k in range(8)], [get(k, 1) for k in range(8)]
    sr = [rr[j] + rr[j + 4] for j in range(4)]
    si = [ii[j] + ii[j + 4] for j in range(4)]
    dr = [rr[j] - rr[j + 4] for j in range(4)]
    di = [ii[j] - ii[j + 4] for j in range(4)]
    half = math.sqrt(0.5)
    re0, im0 = (sr[0] + sr[2]) + (sr[1] + sr[3]), (si[0] + si[2]) + (si[1] + si[3])
    re3, im3 = (sr[0] - sr[2]) - (si[1] - si[3]), (si[0] - si[2]) + (sr[1] - sr[3])
    p, q = (dr[1] - dr[3]) * half, (di[1] + di[3]) * half
    r, t = (di[1] - di[3]) * half, (dr[1] + dr[3]) * half
    re2, im2 = (dr[0] + di[2]) + (p + q), (di[0] - dr[2]) + (r - t)
    re1, im1 = (dr[0] - di[2]) + (p - q), (di[0] + dr[2]) + (r + t)
    fields = ((re0, im0), (re1, im1), (re2, im2), (re3, im3))
    return [re * re + (im * im + 0.05) for re, im in fields]


def ratio_and_total(powers, d):
    total = powers[0][d]
    ratio = None
    for first, second in zip(powers[:-1], powers[1:]):
        first, second = first[d], second[d]
        total = total + second
        prod, both = first * second, first + second
        term = prod * lax.rsqrt(prod * (both * both))
        ratio = term if ratio is None else ratio + term
    return ratio, total


def tile_at(step, tiles):
    t = lax.axis_index("tile")
    return (tiles - 1 - step) + t * (2 * step - tiles + 1)


def fused_kernel(
    retina, qblock, bias, spec, scales, joined_out,
    xin, factors, table, wins, trig, steps, perm, da, db, ga, gb, prev, score_acc,
    sent, got, score_sent, score_got, part_sent, part_got, part_near, redge,
    fix_sent, fix_got, fix_near,
    isem, ssem, rsem, csem, dsem, psem, qsem, lsem, esem, fsem,
):
    tiles, repeats, lines, samples = xin.shape
    chunk = perm.shape[0]
    chunks = samples // chunk
    n = score_got.shape[1]
    half = n // 2
    rows = redge.shape[2]
    me, t = lax.axis_index("vol"), lax.axis_index("tile")
    other = 1 - t
    side, place = me // half, me % half
    part = chunk // CLASSES
    cols = repeats * lines

    data, g = (da, db), (ga, gb)

    def load(step):
        at = pl.ds(pl.multiple_of(tile_at(step, tiles) * lines, lines), lines)
        return pltpu.make_async_copy(spec.at[0, :, at, :], xin.at[step], isem.at[step])

    for step in range(tiles):
        load(step).start()
    barrier = pltpu.get_barrier_semaphore()
    for d in range(1, n):
        pl.semaphore_signal(barrier, inc=1, device_id={"vol": (me + d) % n}, device_id_type=MESH)
    pl.semaphore_signal(barrier, inc=1, device_id={"tile": other}, device_id_type=MESH)
    build_trig(wins, trig, steps, perm, samples)
    per = chunk // SB
    for step in range(tiles):
        lane = pl.ds(pl.multiple_of(tile_at(step, tiles) * lines, lines), lines)
        for r in range(repeats):
            block = scales[0, r, :, lane]
            for q in range(chunks):
                factors[step, q, :per, r * lines : (r + 1) * lines] = block[q * per : (q + 1) * per]

    def prepare(step, q):
        at = pl.ds(q * chunk if isinstance(q, int) else pl.multiple_of(q * chunk, chunk), chunk)
        block = xin[step, :, :, at].reshape(cols, chunk)
        moved = lax.dot_general(
            perm[...], block, (((1,), (1,)), ((), ())), preferred_element_type=jnp.float32
        )
        factor = jnp.concatenate(
            [
                jnp.broadcast_to(factors[step, q, h : h + 1, :], (part // per, cols))
                for h in range(per)
            ],
            axis=0,
        )
        to = pl.ds(q * part if isinstance(q, int) else pl.multiple_of(q * part, part), part)
        for k0 in range(CLASSES):
            data[step % 2][k0, to, :] = (moved[k0 * part : (k0 + 1) * part] * factor).astype(
                jnp.bfloat16
            )

    def multiply(step, p, slot, k0):
        g[slot][k0] = jnp.dot(
            table[p, k0], data[step % 2][k0], preferred_element_type=jnp.float32
        )

    sub = lax.broadcasted_iota(jnp.int32, (8, lines), 0)
    backwards = (8 - sub) % 8

    def dec_of(ratio):
        return 1.0 - ratio * (2.0 / (BANDS * (repeats - 1)))

    def struct_of(total):
        return jnp.log(total * (1.0 / (BANDS * repeats)) + 0.05)

    def lanes(r):
        return slice(r * lines, (r + 1) * lines)

    def reduce_last(slot):
        powers = [
            combine(lambda k, c: g[slot][k, HEAD + c * 8 : HEAD + c * 8 + 8, lanes(r)])
            for r in range(repeats)
        ]
        for d in (1, 3):
            ratio, total = ratio_and_total(powers, d)
            ratio = jnp.sum(ratio[:BANDS], axis=0, keepdims=True)
            total = jnp.sum(total[:BANDS], axis=0, keepdims=True)
            prev[d // 2, 0] = jnp.broadcast_to(dec_of(ratio), (8, lines))
            prev[d // 2, 1] = jnp.broadcast_to(struct_of(total), (8, lines))

    def reduce(step, p, slot, i):
        here = tile_at(step, tiles)
        first, last, rated = retina[0, here], retina[1, here], qblock[0, here]
        at = (GROUPS - 1 - i) * 8 if UNROLL == GROUPS else pl.multiple_of((GROUPS - 1 - i) * 8, 8)
        ratios, totals = [None] * NDB, [None] * NDB
        for b in range(BANDS):
            powers = [
                combine(lambda k, c: g[slot][k, pl.ds((b * 2 + c) * PART + at, 8), lanes(r)])
                for r in range(repeats)
            ]
            for d in range(NDB):
                ratio, total = ratio_and_total(powers, d)
                ratios[d] = ratio if b == 0 else ratios[d] + ratio
                totals[d] = total if b == 0 else totals[d] + total
        score = score_acc[...]
        for d in range(NDB):
            dec, struct = dec_of(ratios[d]), struct_of(totals[d])
            to = at
            if d % 2:
                low_dec, low_struct = prev[d // 2, 0], prev[d // 2, 1]
                prev[d // 2, 0] = dec
                prev[d // 2, 1] = struct
                dec = jnp.where(sub == 0, low_dec, jnp.take_along_axis(dec, backwards, axis=0))
                struct = jnp.where(
                    sub == 0, low_struct, jnp.take_along_axis(struct, backwards, axis=0)
                )
                to = i * 8 if UNROLL == GROUPS else pl.multiple_of(i * 8, 8)
            inside = (first <= d) & (d <= last)
            score = score + jnp.where(rated == d, struct, 0.0)
            sent[step, p, d, 0, pl.ds(to, 8), :] = jnp.where(inside, dec, 0.0)
            sent[step, p, d, 1, pl.ds(to, 8), :] = jnp.where(inside, struct, 0.0)
        score_acc[...] = score

    def goes_to(p, d):
        depth = d * DBLK + (DBLK - PART - p * PART if d % 2 else p * PART)
        u = depth // rows
        return u // half, u % half, depth % rows

    def maps(step, p, d):
        far, target, at = goes_to(p, d)
        return pltpu.make_async_remote_copy(
            src_ref=sent.at[step, p, d],
            dst_ref=got.at[step, place, far, :, pl.ds(at, PART), :],
            send_sem=ssem.at[step], recv_sem=rsem.at[step, place],
            device_id={"vol": side * half + target}, device_id_type=MESH,
        )

    def own_maps(step, p, d):
        far, target, at = goes_to(p, d)
        return pltpu.make_async_copy(
            sent.at[step, p, d], got.at[step, place, far, :, pl.ds(at, PART), :],
            lsem.at[0, step],
        )

    def arrived(step, source):
        return pltpu.make_async_remote_copy(
            src_ref=got.at[step, source], dst_ref=got.at[step, source],
            send_sem=ssem.at[step], recv_sem=rsem.at[step, source],
            device_id={"vol": side * half + source}, device_id_type=MESH,
        )

    def all_sent(step):
        those = got.at[step, pl.ds(0, half - 1)]
        return pltpu.make_async_remote_copy(
            src_ref=those, dst_ref=those,
            send_sem=ssem.at[step], recv_sem=rsem.at[step, 0],
            device_id={"vol": (me + 1) % n}, device_id_type=MESH,
        )

    def own_arrived(step):
        return pltpu.make_async_copy(got.at[step, place], got.at[step, place], lsem.at[0, step])

    def score_to(step, d):
        return pltpu.make_async_remote_copy(
            src_ref=score_sent.at[step], dst_ref=score_got.at[step, me],
            send_sem=csem.at[step], recv_sem=dsem.at[step, me],
            device_id={"vol": (me + d) % n}, device_id_type=MESH,
        )

    def group_score_from(step, d):
        source = side * half + (place + d) % half
        return pltpu.make_async_remote_copy(
            src_ref=score_sent.at[step], dst_ref=score_got.at[step, source],
            send_sem=csem.at[step], recv_sem=dsem.at[step, source],
            device_id={"vol": source}, device_id_type=MESH,
        )

    def other_score_from(step, d):
        source = (1 - side) * half + (place + d) % half
        return pltpu.make_async_remote_copy(
            src_ref=score_sent.at[step], dst_ref=score_got.at[step, source],
            send_sem=csem.at[step], recv_sem=dsem.at[step, source],
            device_id={"vol": source}, device_id_type=MESH,
        )

    def scores_sent(step):
        those = score_got.at[step, pl.ds(0, n - 1)]
        return pltpu.make_async_remote_copy(
            src_ref=those, dst_ref=those,
            send_sem=csem.at[step], recv_sem=dsem.at[step, 0],
            device_id={"vol": (me + 1) % n}, device_id_type=MESH,
        )

    def partial(step):
        return pltpu.make_async_remote_copy(
            src_ref=part_sent.at[step], dst_ref=part_got.at[step],
            send_sem=psem.at[step], recv_sem=qsem.at[step],
            device_id={"vol": (1 - side) * half + place}, device_id_type=MESH,
        )

    fixes = pltpu.make_async_remote_copy(
        src_ref=fix_sent, dst_ref=fix_got, send_sem=fsem.at[0], recv_sem=fsem.at[1],
        device_id={"vol": (1 - side) * half + place}, device_id_type=MESH,
    )

    edge = pltpu.make_async_remote_copy(
        src_ref=got.at[0, :, :, 0], dst_ref=redge,
        send_sem=esem.at[0], recv_sem=esem.at[1],
        device_id={"tile": other}, device_id_type=MESH,
    )

    def send_part(step, p):
        for d in range(NDB):
            _, target, _ = goes_to(p, d)

            @pl.when(place != target)
            def _():
                maps(step, p, d).start()

            @pl.when(place == target)
            def _():
                own_maps(step, p, d).start()

    lane = lax.broadcasted_iota(jnp.int32, (8, lines), 1)
    facing = jnp.where(t == 0, lane, lines - 1 - lane) < 2

    def send_score(step):
        total = jnp.sum(score_acc[...], axis=0, keepdims=True)
        mean = jnp.sum(total, axis=1, keepdims=True) * (1.0 / (DBLK * lines))
        mean = mean + bias[0, tile_at(step, tiles)]
        score_sent[step] = jnp.broadcast_to(mean, (8, lines))
        for d in range(1, n):
            score_to(step, d).start()
        pltpu.make_async_copy(
            score_sent.at[step], score_got.at[step, me], lsem.at[1, step]
        ).start()

    def arrive(step):
        own_arrived(step).wait()
        pltpu.make_async_copy(
            score_sent.at[step], score_got.at[step, me], lsem.at[1, step]
        ).wait()
        for d in range(1, half):
            group_score_from(step, d).wait_recv()
        for d in range(1, half):
            arrived(step, (place + d) % half).wait_recv()

    def group_weights(step, at):
        ratings = [score_got[step, at * half + v, :1, :] for v in range(half)]
        top = functools.reduce(jnp.maximum, ratings)
        return top, [jnp.exp(x - top) for x in ratings]

    def shares(step):
        near_top, near_weights = group_weights(step, side)
        far_top, far_weights = group_weights(step, 1 - side)
        top = jnp.maximum(near_top, far_top)
        near, far = jnp.exp(near_top - top), jnp.exp(far_top - top)
        total = near * functools.reduce(jnp.add, near_weights)
        total = total + far * functools.reduce(jnp.add, far_weights)
        return near / total, far / total

    def smooth_of(step, v, to, at, with_next):
        own = got[step, v, to, 0, pl.ds(at, 8), :]
        if step:
            inner = got[step - 1, v, to, 0, pl.ds(at, 8), :]
        else:
            inner = redge[v, to, pl.ds(at, 8), :]
        outer = got[step + 1, v, to, 0, pl.ds(at, 8), :] if with_next else 0.0
        near_right = jnp.where(lane < lines // 2, jnp.where(t == 0, inner, outer), own)
        near_left = jnp.where(lane < lines // 2, own, jnp.where(t == 0, outer, inner))
        right2 = pltpu.roll(jnp.where(lane >= lines - 2, near_left, own), 2, 1)
        right1 = pltpu.roll(jnp.where(lane >= lines - 1, near_left, own), 1, 1)
        left1 = pltpu.roll(jnp.where(lane < 1, near_right, own), lines - 1, 1)
        left2 = pltpu.roll(jnp.where(lane < 2, near_right, own), lines - 2, 1)
        return (
            (right2 + left2) * (1.0 / 9.0) + (right1 + left1) * (2.0 / 9.0) + own * (3.0 / 9.0)
        )

    def add_up(step):
        _, weights = group_weights(step, side)
        for far in range(2):
            to = 1 - side if far else side
            store = part_sent if far else part_near
            for at in range(0, rows, 8):
                ang = square = joined = 0.0
                for v in range(half):
                    smooth = smooth_of(step, v, to, at, False)
                    ws = weights[v] * smooth
                    ang = ang + ws
                    square = square + ws * smooth
                    joined = joined + weights[v] * got[step, v, to, 1, pl.ds(at, 8), :]
                store[step, 0, at : at + 8, :] = ang
                store[step, 1, at : at + 8, :] = square
                store[step, 2, at : at + 8, :] = joined
        partial(step).start()

    def fix_at(step, k, i):
        return (step * 2 + k) * (rows // 8) + i

    assert 2 * fix_at(max(tiles - 2, 0), 1, rows // 8 - 1) + 2 <= lines

    def fix_up(step):
        _, weights = group_weights(step, side)
        for far in range(2):
            to = 1 - side if far else side
            store = fix_sent if far else fix_near
            packed = store[...] if step else jnp.zeros((8, lines), jnp.float32)
            for i in range(rows // 8):
                ang = square = 0.0
                for v in range(half):
                    smooth = smooth_of(step, v, to, i * 8, True)
                    ws = weights[v] * smooth
                    ang = ang + ws
                    square = square + ws * smooth
                for k, value in enumerate((ang, square)):
                    value = jnp.where(t == 0, value, pltpu.roll(value, 2, 1))
                    place_at = fix_at(step, k, i)
                    moved = pltpu.roll(value, 2 * place_at, 1) if place_at else value
                    packed = jnp.where(lane // 2 == place_at, moved, packed)
            store[...] = packed

    load(0).wait()

    def first_pass(k0, carry):
        build_class(table, wins, trig, steps, k0)
        prepare(0, k0)
        return carry

    assert chunks == CLASSES and GROUPS == SPREAD * (chunks // PARTS)
    for k0 in range(CLASSES):
        first_pass(k0, 0)
    for k0 in range(CLASSES):
        multiply(0, PARTS - 1, 0, k0)
    for step in range(1, tiles):
        load(step).wait()
    if tiles > 1:
        for q in range(chunks // PARTS):
            prepare(1, q)

    slot = 0
    each = CLASSES // GROUPS
    for step in range(tiles):
        score_acc[...] = jnp.zeros_like(score_acc)
        reduce_last(slot)
        for turn_at in range(PARTS):
            p = PARTS - 1 - turn_at
            if turn_at + 1 < PARTS:
                following = (step, p - 1)
            elif step + 1 < tiles:
                following = (step + 1, PARTS - 1)
            else:
                following = None

            if turn_at + 1 < PARTS:
                ready, first_chunk = step + 1, (turn_at + 1) * (chunks // PARTS)
            else:
                ready, first_chunk = step + 2, 0
            if ready >= tiles:
                ready = None

            def body(trip, carry):
                for inner_trip in range(UNROLL):
                    i = trip * UNROLL + inner_trip
                    if following is not None:
                        for k in range(each):
                            multiply(*following, 1 - slot, i * each + k)
                    if ready is not None and (inner_trip + 1) % SPREAD == 0:
                        prepare(ready, first_chunk + (trip * UNROLL + inner_trip) // SPREAD)
                    reduce(step, p, slot, i)
                return carry

            if UNROLL == GROUPS:
                body(0, 0)
            else:
                lax.fori_loop(0, GROUPS // UNROLL, body, 0)
            slot = 1 - slot
            if step == 0 and turn_at == 0:
                pl.semaphore_wait(barrier, n)
            if turn_at + 1 == PARTS:
                send_score(step)
            send_part(step, p)
            if step == 1 and turn_at == 1:
                arrive(0)
                edge.start()
            if step == 1 and turn_at + 1 == PARTS:
                edge.wait_recv()
                add_up(0)
    if tiles == 1:
        arrive(0)
        edge.start()
        edge.wait_recv()
        add_up(0)
    for step in range(1, tiles):
        arrive(step)
        add_up(step)
        fix_up(step - 1)
    if tiles > 1:
        fixes.start()
    for step in range(tiles):
        for d in range(half):
            other_score_from(step, d).wait_recv()
        partial(step).wait_recv()
        near, far = shares(step)
        at = pl.ds(pl.multiple_of(tile_at(step, tiles) * lines, lines), lines)
        for k in range(3):
            joined_out[k, :, at] = near * part_near[step, k] + far * part_got[step, k]
    if tiles > 1:
        fixes.wait_recv()
        for step in range(tiles - 1):
            near, far = shares(step)
            fixed = near * fix_near[...] + far * fix_got[...]
            at = pl.ds(pl.multiple_of(tile_at(step, tiles) * lines, lines), lines)
            for k in range(2):
                for i in range(rows // 8):
                    moved = pltpu.roll(fixed, (lines - 2 * fix_at(step, k, i)) % lines, 1)
                    moved = jnp.where(t == 0, moved, pltpu.roll(moved, lines - 2, 1))
                    to = pl.ds(i * 8, 8)
                    joined_out[k, to, at] = jnp.where(facing, moved, joined_out[k, to, at])
    for step in range(tiles):
        partial(step).wait_send()
        scores_sent(step).wait_send()
        all_sent(step).wait_send()
    if tiles > 1:
        fixes.wait_send()
    edge.wait_send()


def fused(n, spectra, block_scales, retina, qblock, bias):
    _, repeats, lines, samples = spectra.shape
    tiles = lines // ABLK
    inner = samples // CLASSES
    cols = repeats * ABLK
    rows = DEPTH // n
    half = n // 2
    smem = pl.BlockSpec(memory_space=pltpu.SMEM)
    return pl.pallas_call(
        fused_kernel,
        out_shape=jax.ShapeDtypeStruct((3, rows, lines), jnp.float32),
        in_specs=[
            smem, smem, smem,
            pl.BlockSpec(memory_space=pl.ANY),
            pl.BlockSpec(memory_space=pltpu.VMEM),
        ],
        out_specs=pl.BlockSpec(memory_space=pltpu.VMEM),
        scratch_shapes=[
            pltpu.VMEM((tiles, repeats, ABLK, samples), jnp.bfloat16),
            pltpu.VMEM((tiles, samples // 256, 8, cols), jnp.float32),
            pltpu.VMEM((PARTS, CLASSES, LHS, inner), jnp.bfloat16),
            pltpu.VMEM((CLASSES, 8, inner), jnp.float32),
            pltpu.VMEM((2, DBLK + 8, inner), jnp.float32),
            pltpu.VMEM((2, DBLK + 8, 128), jnp.float32),
            pltpu.VMEM((256, 256), jnp.bfloat16),
            pltpu.VMEM((CLASSES, inner, cols), jnp.bfloat16),
            pltpu.VMEM((CLASSES, inner, cols), jnp.bfloat16),
            pltpu.VMEM((CLASSES, LHS, cols), jnp.float32),
            pltpu.VMEM((CLASSES, LHS, cols), jnp.float32),
            pltpu.VMEM((2, 2, 8, ABLK), jnp.float32),
            pltpu.VMEM((8, ABLK), jnp.float32),
            pltpu.VMEM((tiles, PARTS, NDB, 2, PART, ABLK), jnp.float32),
            pltpu.VMEM((tiles, half, 2, 2, rows, ABLK), jnp.float32),
            pltpu.VMEM((tiles, 8, ABLK), jnp.float32),
            pltpu.VMEM((tiles, n, 8, ABLK), jnp.float32),
            pltpu.VMEM((tiles, 3, rows, ABLK), jnp.float32),
            pltpu.VMEM((tiles, 3, rows, ABLK), jnp.float32),
            pltpu.VMEM((tiles, 3, rows, ABLK), jnp.float32),
            pltpu.VMEM((half, 2, rows, ABLK), jnp.float32),
            pltpu.VMEM((8, ABLK), jnp.float32),
            pltpu.VMEM((8, ABLK), jnp.float32),
            pltpu.VMEM((8, ABLK), jnp.float32),
            pltpu.SemaphoreType.DMA((tiles,)),
            pltpu.SemaphoreType.DMA((tiles,)),
            pltpu.SemaphoreType.DMA((tiles, half)),
            pltpu.SemaphoreType.DMA((tiles,)),
            pltpu.SemaphoreType.DMA((tiles, n)),
            pltpu.SemaphoreType.DMA((tiles,)),
            pltpu.SemaphoreType.DMA((tiles,)),
            pltpu.SemaphoreType.DMA((2, tiles)),
            pltpu.SemaphoreType.DMA((2,)),
            pltpu.SemaphoreType.DMA((2,)),
        ],
        compiler_params=pltpu.CompilerParams(
            vmem_limit_bytes=67043328, collective_id=0, has_side_effects=True
        ),
    )(retina.T, qblock, bias, spectra, block_scales.transpose(0, 1, 3, 2))


def finish_kernel(joined, ang_out, str_out, spread_out):
    ang = joined[0]
    ang_out[...] = ang
    str_out[...] = joined[2]
    spread_out[...] = jnp.sqrt(joined[1] - ang * ang + 0.01)


def finish(joined):
    out = jax.ShapeDtypeStruct(joined.shape[1:], jnp.float32)
    return pl.pallas_call(finish_kernel, out_shape=(out, out, out))(joined)


def solution(mesh):
    n = mesh.shape["vol"]
    assert mesh.shape["tile"] == 2

    def on_device(spectra, block_scales, retina_blocks, quality_block, quality_bias):
        return finish(
            fused(n, spectra, block_scales, retina_blocks, quality_block, quality_bias)
        )

    return jax.shard_map(
        on_device,
        mesh=mesh,
        in_specs=(
            P(("study", "vol"), None, "tile", None),
            P(("study", "vol"), None, "tile", None),
            P(("study", "tile"), None),
            P(("study", "vol"), "tile"),
            P(("study", "vol"), "tile"),
        ),
        out_specs=(
            P(("study", "vol"), "tile"),
            P(("study", "vol"), "tile"),
            P(("study", "vol"), "tile"),
        ),
        check_vma=False,
    )
```

time: 50.2 us -> 45.2 us (0.900)
  Pallas kernels: 49.4 us -> 44.4 us
    pallas_call x1, Pallas kernels: 47.7 us -> 42.7 us  [fused(): pl.pallas_call(fused_kernel, out_shape=jax.ShapeDtypeStruct((3, rows, lin...]
where the time goes in v1:
time: 45.2 us; the launch traced here: 45 us
  Pallas kernels  44.4 us (98%)
  between operations  0.64 us (1%)
    pallas_call x1, Pallas kernels, fused(): pl.pallas_call(fused_kernel, out_shape=jax.ShapeDtypeStruct((3, rows, lin...  42.7 us
    pallas_call x1, Pallas kernels, finish(): return pl.pallas_call(finish_kernel, out_shape=(out, out, out))(joined)  1.67 us

profile of v1, /device:TPU:0, one launch (start us, length us, event | category | flops | bytes accessed | tf_op | source)
XLA Modules:
  0.0 45.0 jit_solution(1246141049131299148)
XLA Ops:
  0.6 42.7 %shard_map.76.joined = f32[3,64,384]{2,1,0:T(8,128)} custom-call(s32[2,3]{1,0:T(2,128)} %bitcast.3, s32[1,3]{1,0:T(1,128)} %qblock.1, f32[1,3]{1,0:T(1,128)} %bias.1, bf16[1,4,384,2048]{3,2,1,0:T(8,128)(2,1)} %spec.1, f32[1,4,16,384]{3,2,1,0:T(8,128)} %bitcast.2), custom_call_target="tpu_custom_call" | custom-call | tf_op jit(solution)/shard_map/pallas_call | solution.py:568
  43.3 1.7 %shard_map.77 = (f32[64,384]{1,0:T(8,128)}, f32[64,384]{1,0:T(8,128)}, f32[64,384]{1,0:T(8,128)}) custom-call(f32[3,64,384]{2,1,0:T(8,128)} %shard_map.76.joined), custom_call_target="tpu_custom_call" | custom-call | tf_op jit(solution)/shard_map/pallas_call | solution.py:628

commit v2 on v1

--- a/solution.py
+++ b/solution.py
@@ -19,10 +19,10 @@
 PART = 32
 PARTS = DBLK // PART
 GROUPS = PART // 8
-UNROLL = 4
 SPREAD = 2
 HEAD = BANDS * 2 * PART
 LHS = HEAD + 16
+SPAN = PART // 2
 
 
 def turn(re, im, cre, cim):
@@ -45,6 +45,7 @@
         g = g / jnp.sqrt(jnp.sum(g * g, keepdims=True))
         for k0 in range(CLASSES):
             wins[k0, b : b + 1, :] = g[k0 : k0 + 1]
+            wins[k0, BANDS + b : BANDS + b + 1, :] = g[k0 : k0 + 1]
     z = lax.broadcasted_iota(jnp.int32, (8, inner), 0)
     k1 = lax.broadcasted_iota(jnp.int32, (8, inner), 1)
     angle = ((CLASSES * k1 * z) % samples).astype(jnp.float32) * unit
@@ -77,18 +78,27 @@
     perm[...] = jnp.where(col == (row % part) * CLASSES + row // part, 1.0, 0.0).astype(jnp.bfloat16)
 
 
+def low_of(p, h):
+    return h * (DBLK // 2) + (PARTS - 1 - p) * SPAN
+
+
 def build_class(table, wins, trig, steps, k0):
     inner = trig.shape[2]
     rows = [wins[k0, b : b + 1, :] for b in range(BANDS)]
     for p in range(PARTS):
-        at = pl.ds(p * PART, PART)
         for c in range(2):
-            value = trig[c, at]
+            value = jnp.concatenate(
+                [trig[c, pl.ds(low_of(p, h), SPAN)] for h in range(2)], axis=0
+            )
             for b in range(BANDS):
                 to = pl.ds((b * 2 + c) * PART, PART)
                 table[p, k0, to, :] = (value * rows[b]).astype(jnp.bfloat16)
     last = pl.ds(DBLK, 8)
-    both = jnp.concatenate([trig[c, last] * wins[k0] for c in range(2)], axis=0)
+    high = lax.broadcasted_iota(jnp.int32, (8, inner), 0) < BANDS
+    middle = pl.ds(DBLK // 2, 1)
+    both = jnp.concatenate(
+        [jnp.where(high, trig[c, last], trig[c, middle]) * wins[k0] for c in range(2)], axis=0
+    )
     for p in range(PARTS):
         table[p, k0, HEAD:LHS, :] = both.astype(jnp.bfloat16)
     for at in range(0, DBLK + 8, 8):
@@ -157,8 +167,7 @@
         at = pl.ds(pl.multiple_of(tile_at(step, tiles) * lines, lines), lines)
         return pltpu.make_async_copy(spec.at[0, :, at, :], xin.at[step], isem.at[step])
 
-    for step in range(tiles):
-        load(step).start()
+    load(0).start()
     barrier = pltpu.get_barrier_semaphore()
     for d in range(1, n):
         pl.semaphore_signal(barrier, inc=1, device_id={"vol": (me + d) % n}, device_id_type=MESH)
@@ -215,15 +224,18 @@
         ]
         for d in (1, 3):
             ratio, total = ratio_and_total(powers, d)
-            ratio = jnp.sum(ratio[:BANDS], axis=0, keepdims=True)
-            total = jnp.sum(total[:BANDS], axis=0, keepdims=True)
-            prev[d // 2, 0] = jnp.broadcast_to(dec_of(ratio), (8, lines))
-            prev[d // 2, 1] = jnp.broadcast_to(struct_of(total), (8, lines))
+            for h, those in enumerate((slice(BANDS, 2 * BANDS), slice(0, BANDS))):
+                dec = dec_of(jnp.sum(ratio[those], axis=0, keepdims=True))
+                struct = struct_of(jnp.sum(total[those], axis=0, keepdims=True))
+                prev[h, d // 2, 0] = jnp.broadcast_to(dec, (8, lines))
+                prev[h, d // 2, 1] = jnp.broadcast_to(struct, (8, lines))
 
     def reduce(step, p, slot, i):
         here = tile_at(step, tiles)
         first, last, rated = retina[0, here], retina[1, here], qblock[0, here]
-        at = (GROUPS - 1 - i) * 8 if UNROLL == GROUPS else pl.multiple_of((GROUPS - 1 - i) * 8, 8)
+        h = i % 2
+        within = SPAN - 8 - i // 2 * 8
+        at = h * SPAN + within
         ratios, totals = [None] * NDB, [None] * NDB
         for b in range(BANDS):
             powers = [
@@ -237,40 +249,41 @@
         score = score_acc[...]
         for d in range(NDB):
             dec, struct = dec_of(ratios[d]), struct_of(totals[d])
-            to = at
+            to = within
             if d % 2:
-                low_dec, low_struct = prev[d // 2, 0], prev[d // 2, 1]
-                prev[d // 2, 0] = dec
-                prev[d // 2, 1] = struct
+                low_dec, low_struct = prev[h, d // 2, 0], prev[h, d // 2, 1]
+                prev[h, d // 2, 0] = dec
+                prev[h, d // 2, 1] = struct
                 dec = jnp.where(sub == 0, low_dec, jnp.take_along_axis(dec, backwards, axis=0))
                 struct = jnp.where(
                     sub == 0, low_struct, jnp.take_along_axis(struct, backwards, axis=0)
                 )
-                to = i * 8 if UNROLL == GROUPS else pl.multiple_of(i * 8, 8)
+                to = SPAN - 8 - within
             inside = (first <= d) & (d <= last)
             score = score + jnp.where(rated == d, struct, 0.0)
-            sent[step, p, d, 0, pl.ds(to, 8), :] = jnp.where(inside, dec, 0.0)
-            sent[step, p, d, 1, pl.ds(to, 8), :] = jnp.where(inside, struct, 0.0)
+            sent[step, p, d % 2, h, d // 2, 0, pl.ds(to, 8), :] = jnp.where(inside, dec, 0.0)
+            sent[step, p, d % 2, h, d // 2, 1, pl.ds(to, 8), :] = jnp.where(inside, struct, 0.0)
         score_acc[...] = score
 
-    def goes_to(p, d):
-        depth = d * DBLK + (DBLK - PART - p * PART if d % 2 else p * PART)
+    def goes_to(p, d, h):
+        low = low_of(p, h)
+        depth = d * DBLK + (DBLK - SPAN - low if d % 2 else low)
         u = depth // rows
-        return u // half, u % half, depth % rows
-
-    def maps(step, p, d):
-        far, target, at = goes_to(p, d)
-        return pltpu.make_async_remote_copy(
-            src_ref=sent.at[step, p, d],
-            dst_ref=got.at[step, place, far, :, pl.ds(at, PART), :],
+        return u % half, depth % rows
+
+    def maps(step, p, d, h):
+        target, at = goes_to(p, d, h)
+        return pltpu.make_async_remote_copy(
+            src_ref=sent.at[step, p, d, h],
+            dst_ref=got.at[step, place, :, :, pl.ds(at, SPAN), :],
             send_sem=ssem.at[step], recv_sem=rsem.at[step, place],
             device_id={"vol": side * half + target}, device_id_type=MESH,
         )
 
-    def own_maps(step, p, d):
-        far, target, at = goes_to(p, d)
+    def own_maps(step, p, d, h):
+        target, at = goes_to(p, d, h)
         return pltpu.make_async_copy(
-            sent.at[step, p, d], got.at[step, place, far, :, pl.ds(at, PART), :],
+            sent.at[step, p, d, h], got.at[step, place, :, :, pl.ds(at, SPAN), :],
             lsem.at[0, step],
         )
 
@@ -342,16 +355,17 @@
     )
 
     def send_part(step, p):
-        for d in range(NDB):
-            _, target, _ = goes_to(p, d)
-
-            @pl.when(place != target)
-            def _():
-                maps(step, p, d).start()
-
-            @pl.when(place == target)
-            def _():
-                own_maps(step, p, d).start()
+        for d in range(2):
+            for h in range(2):
+                target, _ = goes_to(p, d, h)
+
+                @pl.when(place != target)
+                def _():
+                    maps(step, p, d, h).start()
+
+                @pl.when(place == target)
+                def _():
+                    own_maps(step, p, d, h).start()
 
     lane = lax.broadcasted_iota(jnp.int32, (8, lines), 1)
     facing = jnp.where(t == 0, lane, lines - 1 - lane) < 2
@@ -452,20 +466,20 @@
             store[...] = packed
 
     load(0).wait()
-
-    def first_pass(k0, carry):
+    for step in range(1, tiles):
+        load(step).start()
+
+    def first_pass(k0):
         build_class(table, wins, trig, steps, k0)
         prepare(0, k0)
-        return carry
 
     assert chunks == CLASSES and GROUPS == SPREAD * (chunks // PARTS)
     for k0 in range(CLASSES):
-        first_pass(k0, 0)
+        first_pass(k0)
     for k0 in range(CLASSES):
-        multiply(0, PARTS - 1, 0, k0)
-    for step in range(1, tiles):
-        load(step).wait()
+        multiply(0, 0, 0, k0)
     if tiles > 1:
+        load(1).wait()
         for q in range(chunks // PARTS):
             prepare(1, q)
 
@@ -475,11 +489,11 @@
         score_acc[...] = jnp.zeros_like(score_acc)
         reduce_last(slot)
         for turn_at in range(PARTS):
-            p = PARTS - 1 - turn_at
+            p = turn_at
             if turn_at + 1 < PARTS:
-                following = (step, p - 1)
+                following = (step, p + 1)
             elif step + 1 < tiles:
-                following = (step + 1, PARTS - 1)
+                following = (step + 1, 0)
             else:
                 following = None
 
@@ -489,29 +503,26 @@
                 ready, first_chunk = step + 2, 0
             if ready >= tiles:
                 ready = None
-
-            def body(trip, carry):
-                for inner_trip in range(UNROLL):
-                    i = trip * UNROLL + inner_trip
+            elif turn_at + 1 == PARTS:
+                load(ready).wait()
+
+            def body():
+                for i in range(GROUPS):
                     if following is not None:
                         for k in range(each):
                             multiply(*following, 1 - slot, i * each + k)
-                    if ready is not None and (inner_trip + 1) % SPREAD == 0:
-                        prepare(ready, first_chunk + (trip * UNROLL + inner_trip) // SPREAD)
+                    if ready is not None and (i + 1) % SPREAD == 0:
+                        prepare(ready, first_chunk + i // SPREAD)
                     reduce(step, p, slot, i)
-                return carry
-
-            if UNROLL == GROUPS:
-                body(0, 0)
-            else:
-                lax.fori_loop(0, GROUPS // UNROLL, body, 0)
+
+            body()
             slot = 1 - slot
             if step == 0 and turn_at == 0:
                 pl.semaphore_wait(barrier, n)
             if turn_at + 1 == PARTS:
                 send_score(step)
             send_part(step, p)
-            if step == 1 and turn_at == 1:
+            if step == 1 and turn_at == 2:
                 arrive(0)
                 edge.start()
             if step == 1 and turn_at + 1 == PARTS:
@@ -586,9 +597,9 @@
             pltpu.VMEM((CLASSES, inner, cols), jnp.bfloat16),
             pltpu.VMEM((CLASSES, LHS, cols), jnp.float32),
             pltpu.VMEM((CLASSES, LHS, cols), jnp.float32),
-            pltpu.VMEM((2, 2, 8, ABLK), jnp.float32),
+            pltpu.VMEM((2, 2, 2, 8, ABLK), jnp.float32),
             pltpu.VMEM((8, ABLK), jnp.float32),
-            pltpu.VMEM((tiles, PARTS, NDB, 2, PART, ABLK), jnp.float32),
+            pltpu.VMEM((tiles, PARTS, 2, 2, 2, 2, SPAN, ABLK), jnp.float32),
             pltpu.VMEM((tiles, half, 2, 2, rows, ABLK), jnp.float32),
             pltpu.VMEM((tiles, 8, ABLK), jnp.float32),
             pltpu.VMEM((tiles, n, 8, ABLK), jnp.float32),

time: 45.2 us -> 43.9 us (0.971)
  the two profiles are of different devices: /device:TPU:0 before, /device:TPU:10 now
where the time goes in v2:
time: 43.9 us; the launch traced here: 43.7 us
  Pallas kernels  43.1 us (98%)
  between operations  0.64 us (1%)
    pallas_call x1, Pallas kernels, fused(): pl.pallas_call(fused_kernel, out_shape=jax.ShapeDtypeStruct((3, rows, lin...  41.4 us
    pallas_call x1, Pallas kernels, finish(): return pl.pallas_call(finish_kernel, out_shape=(out, out, out))(joined)  1.67 us

profile of v2, /device:TPU:10, one launch (start us, length us, event | category | flops | bytes accessed | tf_op | source)
XLA Modules:
  0.0 43.7 jit_solution(10285774643763699616)
XLA Ops:
  0.6 41.4 %shard_map.76.joined = f32[3,64,384]{2,1,0:T(8,128)} custom-call(s32[2,3]{1,0:T(2,128)} %bitcast.3, s32[1,3]{1,0:T(1,128)} %qblock.1, f32[1,3]{1,0:T(1,128)} %bias.1, bf16[1,4,384,2048]{3,2,1,0:T(8,128)(2,1)} %spec.1, f32[1,4,16,384]{3,2,1,0:T(8,128)} %bitcast.2), custom_call_target="tpu_custom_call" | custom-call | tf_op jit(solution)/shard_map/pallas_call | solution.py:579
  42.0 1.7 %shard_map.77 = (f32[64,384]{1,0:T(8,128)}, f32[64,384]{1,0:T(8,128)}, f32[64,384]{1,0:T(8,128)}) custom-call(f32[3,64,384]{2,1,0:T(8,128)} %shard_map.76.joined), custom_call_target="tpu_custom_call" | custom-call | tf_op jit(solution)/shard_map/pallas_call | solution.py:639
